TPU v7x, 512 devices: a whole 4x4x16 slice. The times are simulated.
512 devices in a mesh: group: 16 (over z), shard: 32 (over y, x, core).
Axes of the slice: x: 4, y: 4, z: 16, core: 2. Of those that a mesh axis runs over, the one named last changes fastest.
Arguments:
- entry_grads: float32 [16, 32, 256, 1280], P('group', 'shard'), may hold values from -800 to 800
- exit_grads: float32 [16, 32, 256, 1024], P('group', 'shard'), may hold values from -800 to 800
- entry_params: float32 [32, 256, 1280], P('shard', 'group'), may hold values from -0.15625 to 0.15625
- exit_params: float32 [32, 256, 1024], P('shard', 'group'), may hold values from -0.15625 to 0.15625
- entry_mean: float32 [32, 256, 1280], P('shard', 'group'), may hold values from -1.5 to 1.5
- exit_mean: float32 [32, 256, 1024], P('shard', 'group'), may hold values from -1.5 to 1.5
- entry_square: float32 [32, 256, 1280], P('shard', 'group'), may hold values from 0.01 to 1
- exit_square: float32 [32, 256, 1024], P('shard', 'group'), may hold values from 0.01 to 1
Outputs:
- entry_master: float32 [32, 256, 1280], P('shard', 'group')
- exit_master: float32 [32, 256, 1024], P('shard', 'group')
- entry_moment: float32 [32, 256, 1280], P('shard', 'group')
- exit_moment: float32 [32, 256, 1024], P('shard', 'group')
- entry_variance: float32 [32, 256, 1280], P('shard', 'group')
- exit_variance: float32 [32, 256, 1024], P('shard', 'group')
- entry_weights: bfloat16 [32, 256, 1280], P('shard')
- exit_weights: bfloat16 [32, 256, 1024], P('shard')
All inputs are finite; a program needn't handle non-finite values.
Results may differ from a plain program's by a relative error of at most 0.0004.
Values may be sent and summed in bfloat16 or wider, within the bound.
No kernel may reach another device: no remote copies, remote signals or barrier semaphores. Data moves between devices by JAX's collectives and lax.ppermute only.
A program may use at most 64 MiB of HBM per device.

v0:
```python
import jax
import jax.numpy as jnp
from jax import lax
from jax.sharding import PartitionSpec as P

beta_first = 0.9
beta_second = 0.95
learn_rate = 0.01
decay_rate = 0.1
epsilon = 1e-08
correct_first = 1.0 - 0.9**40
correct_second = 1.0 - 0.95**40


def adamw_step(params, mean, square, total, clip):
    grads = clip * total
    moment = beta_first * mean + (1.0 - beta_first) * grads
    variance = beta_second * square + (1.0 - beta_second) * grads * grads
    update = moment / correct_first / (jnp.sqrt(variance / correct_second) + epsilon)
    master = params - learn_rate * (update + decay_rate * params)
    return (master, moment, variance)


def sum_everywhere(values):
    axes = ("group", "shard")
    lanes = jnp.sum(values.reshape(-1, 128), axis=0)
    sent = jnp.broadcast_to(lanes, (lax.axis_size(axes), 1, 128))
    return jnp.sum(lax.all_to_all(sent, axes, 0, 0))


def body(
    entry_grads,
    exit_grads,
    entry_params,
    exit_params,
    entry_mean,
    exit_mean,
    entry_square,
    exit_square,
):
    entry_rows_dev = entry_grads.shape[2]
    exit_rows_dev = exit_grads.shape[2]
    entry_width = entry_grads.shape[3]
    exit_width = exit_grads.shape[3]
    entry_local = entry_grads.reshape(entry_rows_dev, entry_width)
    exit_local = exit_grads.reshape(exit_rows_dev, exit_width)
    packed = jnp.concatenate([entry_local, exit_local], axis=1)
    total = lax.psum_scatter(packed, "group", scatter_dimension=0, tiled=True)
    entry_total = total[:, :entry_width]
    exit_total = total[:, entry_width:]
    squares = sum_everywhere(total * total)
    count = (entry_rows_dev * entry_width + exit_rows_dev * exit_width) * lax.axis_size("shard")
    limit = jnp.sqrt(jnp.float32(count))
    clip = jnp.minimum(jnp.float32(1.0), limit / (jnp.sqrt(squares) + 1e-06))
    entry_master, entry_moment, entry_variance = adamw_step(
        entry_params[0], entry_mean[0], entry_square[0], entry_total, clip
    )
    exit_master, exit_moment, exit_variance = adamw_step(
        exit_params[0], exit_mean[0], exit_square[0], exit_total, clip
    )
    entry_round = entry_master.astype(jnp.bfloat16)
    exit_round = exit_master.astype(jnp.bfloat16)
    entry_weights = lax.all_gather(entry_round, "group", axis=0, tiled=True)
    exit_weights = lax.all_gather(exit_round, "group", axis=0, tiled=True)
    return (
        entry_master[None],
        exit_master[None],
        entry_moment[None],
        exit_moment[None],
        entry_variance[None],
        exit_variance[None],
        entry_weights[None],
        exit_weights[None],
    )


def solution(mesh):
    placed = (
        P("group", "shard", None, None),
        P("group", "shard", None, None),
        P("shard", "group", None),
        P("shard", "group", None),
        P("shard", "group", None),
        P("shard", "group", None),
        P("shard", "group", None),
        P("shard", "group", None),
    )
    return jax.shard_map(
        body,
        mesh=mesh,
        in_specs=placed,
        out_specs=(
            P("shard", "group", None),
            P("shard", "group", None),
            P("shard", "group", None),
            P("shard", "group", None),
            P("shard", "group", None),
            P("shard", "group", None),
            P("shard", None, None),
            P("shard", None, None),
        ),
        check_vma=False,
    )
```

profile of v0, /device:TPU:2, one launch (start us, length us, event | category | flops | bytes accessed | tf_op | source)
XLA Modules:
  0.0 204.4 jit_solution(7940237761173604504)
XLA Ops:
  7.2 0.0 reduce-scatter.2.cloned.1.call-start
  7.2 3.2 %pad_maximum_fusion = f32[256,2304]{1,0:T(8,128)} fusion(f32[256,1024]{1,0:T(8,128)} %bitcast.67, f32[256,1280]{1,0:T(8,128)} %bitcast.65), kind=kLoop, calls=%fused_computation | loop fusion | flops 589824 | bytes 4718592 | tf_op jit(solution)/shard_map/concatenate | solution.py:47
  10.4 0.0 copy-start.4
  10.4 0.0 copy-start.5
  10.4 0.0 copy-start.6
  10.4 0.0 copy-start.1
  10.4 0.0 copy-start.2
  10.5 0.0 copy-start.3
  10.5 0.0 reduce-scatter.2.cloned.1.call-update
  10.5 78.5 %reduce-scatter.2.cloned.1.call-done = f32[16,2304]{1,0:T(8,128)} async-done(((f32[256,2304]{1,0:T(8,128)}), f32[16,2304]{1,0:T(8,128)}) %reduce-scatter.2.cloned.1.call-update) | async-done | bytes 147472 | tf_op jit(solution)/shard_map/reduce_scatter | solution.py:48
  89.0 0.0 copy-start
  89.0 1.1 mul.96
  90.1 0.1 reduce_sum.18
  90.2 0.1 broadcast_in_dim.27
  90.3 40.8 %all_to_all.5 = f32[512,1,128]{2,1,0:T(1,128)S(1)} all-to-all(f32[512,1,128]{2,1,0:T(1,128)S(1)} %broadcast_in_dim.27), channel_id=1, replica_groups=mesh['group'=16,'shard'=32] {'group','shard'}, dimensions={0} | all-to-all | bytes 524288 | tf_op jit(solution)/shard_map/all_to_all | solution.py:28
  131.1 0.7 reduce_sum.19
  132.5 0.0 copy-done.4
  132.5 0.0 copy-done.5
  132.5 0.0 copy-done.6
  132.5 1.5 fusion.10
  134.1 30.4 %all_gather.7 = bf16[256,1024]{1,0:T(8,128)(2,1)S(1)} all-gather(bf16[16,1024]{1,0:T(8,128)(2,1)S(1)} %get-tuple-element.8), channel_id=1, replica_groups=mesh['group'=16,'shard'=32] {'group'}, dimensions={0}, use_global_device_ids=true | all-gather | bytes 557056 | tf_op jit(solution)/shard_map/all_gather | solution.py:64
  164.5 0.0 copy-done.1
  164.5 0.0 copy-done.2
  164.5 0.0 copy-done.3
  164.5 0.0 copy-done
  164.5 0.7 fusion.11
  165.2 30.7 %all_gather.6 = bf16[256,1280]{1,0:T(8,128)(2,1)S(1)} all-gather(bf16[16,1280]{1,0:T(8,128)(2,1)S(1)} %get-tuple-element.10), channel_id=1, replica_groups=mesh['group'=16,'shard'=32] {'group'}, dimensions={0}, use_global_device_ids=true | all-gather | bytes 696320 | tf_op jit(solution)/shard_map/all_gather | solution.py:63
  195.9 0.8 copy.19
  196.8 0.8 copy.20
  (1 shorter events, 0.0 us)
Async XLA Ops:
  7.2 81.9 %reduce-scatter.2.cloned.1.call-start = ((), (), s32[]{:S(2)}) async-start(), calls=%async_computation.2 | async-start | bytes 2506752 | tf_op jit(solution)/shard_map/reduce_scatter | solution.py:48
  10.4 122.1 %copy-start.4 = (f32[1,16,1024]{2,1,0:T(8,128)S(1)}, f32[1,16,1024]{2,1,0:T(8,128)}, u32[]{:S(2)}) copy-start(f32[1,16,1024]{2,1,0:T(8,128)} %param.15) | copy-start | bytes 196612
  10.4 122.1 %copy-start.5 = (f32[1,16,1024]{2,1,0:T(8,128)S(1)}, f32[1,16,1024]{2,1,0:T(8,128)}, u32[]{:S(2)}) copy-start(f32[1,16,1024]{2,1,0:T(8,128)} %param.13) | copy-start | bytes 196612
  10.4 122.1 %copy-start.6 = (f32[1,16,1024]{2,1,0:T(8,128)S(1)}, f32[1,16,1024]{2,1,0:T(8,128)}, u32[]{:S(2)}) copy-start(f32[1,16,1024]{2,1,0:T(8,128)} %param.11) | copy-start | bytes 196612
  10.4 154.1 %copy-start.1 = (f32[1,16,1280]{2,1,0:T(8,128)S(1)}, f32[1,16,1280]{2,1,0:T(8,128)}, u32[]{:S(2)}) copy-start(f32[1,16,1280]{2,1,0:T(8,128)} %param.14) | copy-start | bytes 245764
  10.4 154.1 %copy-start.2 = (f32[1,16,1280]{2,1,0:T(8,128)S(1)}, f32[1,16,1280]{2,1,0:T(8,128)}, u32[]{:S(2)}) copy-start(f32[1,16,1280]{2,1,0:T(8,128)} %param.12) | copy-start | bytes 245764
  10.5 154.1 %copy-start.3 = (f32[1,16,1280]{2,1,0:T(8,128)S(1)}, f32[1,16,1280]{2,1,0:T(8,128)}, u32[]{:S(2)}) copy-start(f32[1,16,1280]{2,1,0:T(8,128)} %param.10) | copy-start | bytes 245764
  89.0 75.5 %copy-start = (f32[16,2304]{1,0:T(8,128)S(1)}, f32[16,2304]{1,0:T(8,128)}, u32[]{:S(2)}) copy-start(f32[16,2304]{1,0:T(8,128)} %reduce-scatter.2.cloned.1.call-done) | copy-start | bytes 442372
Sparse Core Ops, SparseCore 0:
  10.8 78.1 reduce-scatter.1
where the time goes:
time: 205 us; the launch traced here: 204 us
  blocking collectives  102 us (50%)
  waiting for transfers between devices  78.6 us (38%)
  between operations  14.8 us (7%)
  other arithmetic  7.27 us (4%)
    reduce_scatter x1, waiting for transfers between devices, body(): total = lax.psum_scatter(packed, 'group', scatter_dimension=0, tiled=True)  78.5 us
    all_to_all x1, blocking collectives, sum_everywhere(): return jnp.sum(lax.all_to_all(sent, axes, 0, 0))  40.8 us
    all_gather x1, blocking collectives, body(): entry_weights = lax.all_gather(entry_round, 'group', axis=0, tiled=True)  30.7 us
    all_gather x1, blocking collectives, body(): exit_weights = lax.all_gather(exit_round, 'group', axis=0, tiled=True)  30.4 us
  transfers between devices with their start and end apart: 1, of which 1 were waited for; matrix products, arithmetic and copies ran while one was open for 0% of the time, Pallas kernels for 0%

commit v1 on v0

--- a/solution.py
+++ b/solution.py
@@ -10,6 +10,27 @@
 epsilon = 1e-08
 correct_first = 1.0 - 0.9**40
 correct_second = 1.0 - 0.95**40
+
+
+def collect(x, axis, dim):
+    size, index, span = (lax.axis_size(axis), lax.axis_index(axis), x.shape[dim])
+    right = [(i, (i + 1) % size) for i in range(size)]
+    behind = [(i, (i - 1) % size) for i in range(size)]
+    out = jnp.zeros((*x.shape[:dim], size * span, *x.shape[dim + 1 :]), x.dtype)
+    out = lax.dynamic_update_slice_in_dim(out, x, index * span, axis=dim)
+    from_left = from_right = x
+    halfway = size // 2
+    for turn in range(1, halfway + 1):
+        from_left = lax.ppermute(from_left, axis, right)
+        out = lax.dynamic_update_slice_in_dim(
+            out, from_left, (index - turn) % size * span, axis=dim
+        )
+        if turn < size - halfway:
+            from_right = lax.ppermute(from_right, axis, behind)
+            out = lax.dynamic_update_slice_in_dim(
+                out, from_right, (index + turn) % size * span, axis=dim
+            )
+    return out
 
 
 def adamw_step(params, mean, square, total, clip):
@@ -61,7 +82,7 @@
     entry_round = entry_master.astype(jnp.bfloat16)
     exit_round = exit_master.astype(jnp.bfloat16)
     entry_weights = lax.all_gather(entry_round, "group", axis=0, tiled=True)
-    exit_weights = lax.all_gather(exit_round, "group", axis=0, tiled=True)
+    exit_weights = collect(exit_round, "group", 0)
     return (
         entry_master[None],
         exit_master[None],

time: 205 us -> 231 us (1.13)
  the two profiles are of different devices: /device:TPU:2 before, /device:TPU:8 now
where the time goes in v1:
time: 231 us
  waiting for transfers between devices  107 us (46%)
  starting transfers between devices  68.1 us (29%)
  blocking collectives  30.3 us (13%)
  between operations  15.5 us (7%)
  other arithmetic  7.13 us (3%)
    reduce_scatter x1, waiting for transfers between devices, body(): total = lax.psum_scatter(packed, 'group', scatter_dimension=0, tiled=True)  78.6 us
    ppermute x7, starting transfers between devices, collect(): from_right = lax.ppermute(from_right, axis, behind)  33.7 us
    all_gather x1, blocking collectives, body(): entry_weights = lax.all_gather(entry_round, 'group', axis=0, tiled=True)  30.3 us
    all_to_all x1, waiting for transfers between devices, sum_everywhere(): return jnp.sum(lax.all_to_all(sent, axes, 0, 0))  23.6 us
    ppermute x8, starting transfers between devices, collect(): from_left = lax.ppermute(from_left, axis, right)  17.6 us
    all_to_all x1, starting transfers between devices, sum_everywhere(): return jnp.sum(lax.all_to_all(sent, axes, 0, 0))  16.8 us
    ppermute x8, waiting for transfers between devices, collect(): from_left = lax.ppermute(from_left, axis, right)  5.06 us
  transfers between devices with their start and end apart: 17, of which 3 were waited for; matrix products, arithmetic and copies ran while one was open for 1% of the time, Pallas kernels for 0%

profile of v1, /device:TPU:8, one launch (start us, length us, event | category | flops | bytes accessed | tf_op | source)
XLA Modules:
  0.0 230.5 jit_solution(14241081796049920748)
XLA Ops:
  7.2 0.0 reduce-scatter.2.cloned.1.call-start
  7.2 3.2 %pad_maximum_fusion = f32[256,2304]{1,0:T(8,128)} fusion(f32[256,1024]{1,0:T(8,128)} %bitcast.97, f32[256,1280]{1,0:T(8,128)} %bitcast.95), kind=kLoop, calls=%fused_computation | loop fusion | flops 589824 | bytes 4718592 | tf_op jit(solution)/shard_map/concatenate | solution.py:68
  10.5 0.0 copy-start.5
  10.5 0.0 copy-start.6
  10.5 0.0 reduce-scatter.2.cloned.1.call-update
  10.5 78.6 %reduce-scatter.2.cloned.1.call-done = f32[16,2304]{1,0:T(8,128)} async-done(((f32[256,2304]{1,0:T(8,128)}), f32[16,2304]{1,0:T(8,128)}) %reduce-scatter.2.cloned.1.call-update) | async-done | bytes 147472 | tf_op jit(solution)/shard_map/reduce_scatter | solution.py:69
  89.1 1.1 mul.144
  90.2 0.1 reduce_sum.18
  90.3 0.8 broadcast_in_dim.60
  91.1 16.8 %all-to-all-start = ((f32[512,1,128]{2,1,0:T(1,128)}), f32[512,1,128]{2,1,0:T(1,128)S(1)}, u32[]{:S(2)}, u32[]{:S(2)}) async-start(f32[512,1,128]{2,1,0:T(1,128)} %broadcast_in_dim.60), calls=%async_computation.1 | async-start | bytes 524288 | tf_op jit(solution)/shard_map/all_to_all | solution.py:49
  108.3 23.6 %all-to-all-done = f32[512,1,128]{2,1,0:T(1,128)S(1)} async-done(((f32[512,1,128]{2,1,0:T(1,128)}), f32[512,1,128]{2,1,0:T(1,128)S(1)}, u32[]{:S(2)}, u32[]{:S(2)}) %all-to-all-start) | async-done | bytes 262176 | tf_op jit(solution)/shard_map/all_to_all | solution.py:49
  131.9 0.7 reduce_sum.19
  133.3 0.1 broadcast_in_dim.68
  133.4 0.7 bitcast_dynamic-update-slice_fusion.15
  134.1 2.8 %collective-permute-start = (bf16[16,1024]{1,0:T(8,128)(2,1)S(1)}, bf16[16,1024]{1,0:T(8,128)(2,1)S(1)}, u32[]{:S(2)}, u32[]{:S(2)}) collective-permute-start(bf16[16,1024]{1,0:T(8,128)(2,1)S(1)} %get-tuple-element.9), channel_id=1, source_target_pairs={{0,32},{32,64},{64,96},{96,128},{128,160},{160,192},{192,224},{224... | collective-permute-start | bytes 98312 | tf_op jit(solution)/shard_map/ppermute | solution.py:24
  136.9 4.3 %collective-permute-start.1 = (bf16[16,1024]{1,0:T(8,128)(2,1)S(1)}, bf16[16,1024]{1,0:T(8,128)(2,1)S(1)}, u32[]{:S(2)}, u32[]{:S(2)}) collective-permute-start(bf16[16,1024]{1,0:T(8,128)(2,1)S(1)} %get-tuple-element.9), channel_id=1, source_target_pairs={{0,480},{32,0},{64,32},{96,64},{128,96},{160,128},{192,160},{224,1... | collective-permute-start | bytes 98312 | tf_op jit(solution)/shard_map/ppermute | solution.py:29
  141.2 0.7 fusion.10
  141.9 30.3 %all_gather.3 = bf16[256,1280]{1,0:T(8,128)(2,1)S(1)} all-gather(bf16[16,1280]{1,0:T(8,128)(2,1)S(1)} %get-tuple-element.11), channel_id=1, replica_groups=mesh['group'=16,'shard'=32] {'group'}, dimensions={0}, use_global_device_ids=true | all-gather | bytes 696320 | tf_op jit(solution)/shard_map/all_gather | solution.py:84
  172.2 0.7 fusion.9
  172.9 0.0 collective-permute-done
  172.9 3.2 %collective-permute-start.2 = (bf16[16,1024]{1,0:T(8,128)(2,1)S(1)}, bf16[16,1024]{1,0:T(8,128)(2,1)S(1)}, u32[]{:S(2)}, u32[]{:S(2)}) collective-permute-start(bf16[16,1024]{1,0:T(8,128)(2,1)S(1)} %collective-permute-done), channel_id=1, source_target_pairs={{0,32},{32,64},{64,96},{96,128},{128,160},{160,192},{192,224},{224... | collective-permute-start | bytes 98312 | tf_op jit(solution)/shard_map/ppermute | solution.py:24
  176.1 0.0 collective-permute-done.1
  176.1 3.8 %collective-permute-start.3 = (bf16[16,1024]{1,0:T(8,128)(2,1)S(1)}, bf16[16,1024]{1,0:T(8,128)(2,1)S(1)}, u32[]{:S(2)}, u32[]{:S(2)}) collective-permute-start(bf16[16,1024]{1,0:T(8,128)(2,1)S(1)} %collective-permute-done.1), channel_id=1, source_target_pairs={{0,480},{32,0},{64,32},{96,64},{128,96},{160,128},{192,160},{224,1... | collective-permute-start | bytes 98312 | tf_op jit(solution)/shard_map/ppermute | solution.py:29
  180.0 0.0 collective-permute-done.2
  180.0 2.0 collective-permute-start.4
  182.0 0.0 collective-permute-done.3
  182.0 5.0 %collective-permute-start.5 = (bf16[16,1024]{1,0:T(8,128)(2,1)S(1)}, bf16[16,1024]{1,0:T(8,128)(2,1)S(1)}, u32[]{:S(2)}, u32[]{:S(2)}) collective-permute-start(bf16[16,1024]{1,0:T(8,128)(2,1)S(1)} %collective-permute-done.3), channel_id=1, source_target_pairs={{0,480},{32,0},{64,32},{96,64},{128,96},{160,128},{192,160},{224,1... | collective-permute-start | bytes 98312 | tf_op jit(solution)/shard_map/ppermute | solution.py:29
  187.1 0.0 collective-permute-done.4
  187.1 1.9 collective-permute-start.6
  189.1 0.0 collective-permute-done.5
  189.1 5.1 %collective-permute-start.7 = (bf16[16,1024]{1,0:T(8,128)(2,1)S(1)}, bf16[16,1024]{1,0:T(8,128)(2,1)S(1)}, u32[]{:S(2)}, u32[]{:S(2)}) collective-permute-start(bf16[16,1024]{1,0:T(8,128)(2,1)S(1)} %collective-permute-done.5), channel_id=1, source_target_pairs={{0,480},{32,0},{64,32},{96,64},{128,96},{160,128},{192,160},{224,1... | collective-permute-start | bytes 98312 | tf_op jit(solution)/shard_map/ppermute | solution.py:29
  194.2 0.0 collective-permute-done.6
  194.2 1.9 collective-permute-start.8
  196.2 0.0 collective-permute-done.7
  196.2 5.1 %collective-permute-start.9 = (bf16[16,1024]{1,0:T(8,128)(2,1)S(1)}, bf16[16,1024]{1,0:T(8,128)(2,1)S(1)}, u32[]{:S(2)}, u32[]{:S(2)}) collective-permute-start(bf16[16,1024]{1,0:T(8,128)(2,1)S(1)} %collective-permute-done.7), channel_id=1, source_target_pairs={{0,480},{32,0},{64,32},{96,64},{128,96},{160,128},{192,160},{224,1... | collective-permute-start | bytes 98312 | tf_op jit(solution)/shard_map/ppermute | solution.py:29
  201.4 0.0 collective-permute-done.8
  201.4 1.9 collective-permute-start.10
  203.3 0.0 collective-permute-done.9
  203.3 5.1 %collective-permute-start.11 = (bf16[16,1024]{1,0:T(8,128)(2,1)S(1)}, bf16[16,1024]{1,0:T(8,128)(2,1)S(1)}, u32[]{:S(2)}, u32[]{:S(2)}) collective-permute-start(bf16[16,1024]{1,0:T(8,128)(2,1)S(1)} %collective-permute-done.9), channel_id=1, source_target_pairs={{0,480},{32,0},{64,32},{96,64},{128,96},{160,128},{192,160},{224,1... | collective-permute-start | bytes 98312 | tf_op jit(solution)/shard_map/ppermute | solution.py:29
  208.5 1.9 collective-permute-start.12
  210.4 0.0 collective-permute-done.11
  210.4 5.1 %collective-permute-start.13 = (bf16[16,1024]{1,0:T(8,128)(2,1)S(1)}, bf16[16,1024]{1,0:T(8,128)(2,1)S(1)}, u32[]{:S(2)}, u32[]{:S(2)}) collective-permute-start(bf16[16,1024]{1,0:T(8,128)(2,1)S(1)} %collective-permute-done.11), channel_id=1, source_target_pairs={{0,480},{32,0},{64,32},{96,64},{128,96},{160,128},{192,160},{224,1... | collective-permute-start | bytes 98312 | tf_op jit(solution)/shard_map/ppermute | solution.py:29
  215.6 0.0 collective-permute-done.12
  215.6 1.9 collective-permute-start.14
  217.6 0.0 collective-permute-done.13
  217.6 5.0 %collective-permute-done.14 = bf16[16,1024]{1,0:T(8,128)(2,1)S(1)} collective-permute-done((bf16[16,1024]{1,0:T(8,128)(2,1)S(1)}, bf16[16,1024]{1,0:T(8,128)(2,1)S(1)}, u32[]{:S(2)}, u32[]{:S(2)}) %collective-permute-start.14) | collective-permute-done | bytes 32800 | tf_op jit(solution)/shard_map/ppermute | solution.py:24
  222.7 0.9 copy.34
  223.5 0.1 copy-done.1
  (30 shorter events, 0.2 us)
Async XLA Ops:
  7.2 82.0 %reduce-scatter.2.cloned.1.call-start = ((), (), s32[]{:S(2)}) async-start(), calls=%async_computation.2 | async-start | bytes 2506752 | tf_op jit(solution)/shard_map/reduce_scatter | solution.py:69
  10.4 122.9 %copy-start.2 = (f32[1,16,1024]{2,1,0:T(8,128)S(1)}, f32[1,16,1024]{2,1,0:T(8,128)}, u32[]{:S(2)}) copy-start(f32[1,16,1024]{2,1,0:T(8,128)} %param.15) | copy-start | bytes 196612
  10.5 122.9 %copy-start.3 = (f32[1,16,1024]{2,1,0:T(8,128)S(1)}, f32[1,16,1024]{2,1,0:T(8,128)}, u32[]{:S(2)}) copy-start(f32[1,16,1024]{2,1,0:T(8,128)} %param.13) | copy-start | bytes 196612
  10.5 122.9 %copy-start.7 = (f32[1,16,1024]{2,1,0:T(8,128)S(1)}, f32[1,16,1024]{2,1,0:T(8,128)}, u32[]{:S(2)}) copy-start(f32[1,16,1024]{2,1,0:T(8,128)} %param.11) | copy-start | bytes 196612
  10.5 130.7 %copy-start.4 = (f32[1,16,1280]{2,1,0:T(8,128)S(1)}, f32[1,16,1280]{2,1,0:T(8,128)}, u32[]{:S(2)}) copy-start(f32[1,16,1280]{2,1,0:T(8,128)} %param.14) | copy-start | bytes 245764
  10.5 130.7 %copy-start.5 = (f32[1,16,1280]{2,1,0:T(8,128)S(1)}, f32[1,16,1280]{2,1,0:T(8,128)}, u32[]{:S(2)}) copy-start(f32[1,16,1280]{2,1,0:T(8,128)} %param.12) | copy-start | bytes 245764
  10.5 130.7 %copy-start.6 = (f32[1,16,1280]{2,1,0:T(8,128)S(1)}, f32[1,16,1280]{2,1,0:T(8,128)}, u32[]{:S(2)}) copy-start(f32[1,16,1280]{2,1,0:T(8,128)} %param.10) | copy-start | bytes 245764
  89.1 44.2 %copy-start = (f32[16,2304]{1,0:T(8,128)S(1)}, f32[16,2304]{1,0:T(8,128)}, u32[]{:S(2)}) copy-start(f32[16,2304]{1,0:T(8,128)} %reduce-scatter.2.cloned.1.call-done) | copy-start | bytes 442372
  91.1 40.8 %all-to-all-start = ((f32[512,1,128]{2,1,0:T(1,128)}), f32[512,1,128]{2,1,0:T(1,128)S(1)}, u32[]{:S(2)}, u32[]{:S(2)}) async-start(f32[512,1,128]{2,1,0:T(1,128)} %broadcast_in_dim.60), calls=%async_computation.1 | async-start | bytes 524288 | tf_op jit(solution)/shard_map/all_to_all | solution.py:49
  134.1 38.8 %collective-permute-start = (bf16[16,1024]{1,0:T(8,128)(2,1)S(1)}, bf16[16,1024]{1,0:T(8,128)(2,1)S(1)}, u32[]{:S(2)}, u32[]{:S(2)}) collective-permute-start(bf16[16,1024]{1,0:T(8,128)(2,1)S(1)} %get-tuple-element.9), channel_id=1, source_target_pairs={{0,32},{32,64},{64,96},{96,128},{128,160},{160,192},{192,224},{224... | collective-permute-start | bytes 98312 | tf_op jit(solution)/shard_map/ppermute | solution.py:24
  136.9 39.2 %collective-permute-start.1 = (bf16[16,1024]{1,0:T(8,128)(2,1)S(1)}, bf16[16,1024]{1,0:T(8,128)(2,1)S(1)}, u32[]{:S(2)}, u32[]{:S(2)}) collective-permute-start(bf16[16,1024]{1,0:T(8,128)(2,1)S(1)} %get-tuple-element.9), channel_id=1, source_target_pairs={{0,480},{32,0},{64,32},{96,64},{128,96},{160,128},{192,160},{224,1... | collective-permute-start | bytes 98312 | tf_op jit(solution)/shard_map/ppermute | solution.py:29
  172.9 7.1 %collective-permute-start.2 = (bf16[16,1024]{1,0:T(8,128)(2,1)S(1)}, bf16[16,1024]{1,0:T(8,128)(2,1)S(1)}, u32[]{:S(2)}, u32[]{:S(2)}) collective-permute-start(bf16[16,1024]{1,0:T(8,128)(2,1)S(1)} %collective-permute-done), channel_id=1, source_target_pairs={{0,32},{32,64},{64,96},{96,128},{128,160},{160,192},{192,224},{224... | collective-permute-start | bytes 98312 | tf_op jit(solution)/shard_map/ppermute | solution.py:24
  176.1 5.9 %collective-permute-start.3 = (bf16[16,1024]{1,0:T(8,128)(2,1)S(1)}, bf16[16,1024]{1,0:T(8,128)(2,1)S(1)}, u32[]{:S(2)}, u32[]{:S(2)}) collective-permute-start(bf16[16,1024]{1,0:T(8,128)(2,1)S(1)} %collective-permute-done.1), channel_id=1, source_target_pairs={{0,480},{32,0},{64,32},{96,64},{128,96},{160,128},{192,160},{224,1... | collective-permute-start | bytes 98312 | tf_op jit(solution)/shard_map/ppermute | solution.py:29
  180.0 7.1 %collective-permute-start.4 = (bf16[16,1024]{1,0:T(8,128)(2,1)S(1)}, bf16[16,1024]{1,0:T(8,128)(2,1)S(1)}, u32[]{:S(2)}, u32[]{:S(2)}) collective-permute-start(bf16[16,1024]{1,0:T(8,128)(2,1)S(1)} %collective-permute-done.2), channel_id=1, source_target_pairs={{0,32},{32,64},{64,96},{96,128},{128,160},{160,192},{192,224},{224... | collective-permute-start | bytes 98312 | tf_op jit(solution)/shard_map/ppermute | solution.py:24
  182.0 7.0 %collective-permute-start.5 = (bf16[16,1024]{1,0:T(8,128)(2,1)S(1)}, bf16[16,1024]{1,0:T(8,128)(2,1)S(1)}, u32[]{:S(2)}, u32[]{:S(2)}) collective-permute-start(bf16[16,1024]{1,0:T(8,128)(2,1)S(1)} %collective-permute-done.3), channel_id=1, source_target_pairs={{0,480},{32,0},{64,32},{96,64},{128,96},{160,128},{192,160},{224,1... | collective-permute-start | bytes 98312 | tf_op jit(solution)/shard_map/ppermute | solution.py:29
  187.1 7.1 %collective-permute-start.6 = (bf16[16,1024]{1,0:T(8,128)(2,1)S(1)}, bf16[16,1024]{1,0:T(8,128)(2,1)S(1)}, u32[]{:S(2)}, u32[]{:S(2)}) collective-permute-start(bf16[16,1024]{1,0:T(8,128)(2,1)S(1)} %collective-permute-done.4), channel_id=1, source_target_pairs={{0,32},{32,64},{64,96},{96,128},{128,160},{160,192},{192,224},{224... | collective-permute-start | bytes 98312 | tf_op jit(solution)/shard_map/ppermute | solution.py:24
  189.1 7.1 %collective-permute-start.7 = (bf16[16,1024]{1,0:T(8,128)(2,1)S(1)}, bf16[16,1024]{1,0:T(8,128)(2,1)S(1)}, u32[]{:S(2)}, u32[]{:S(2)}) collective-permute-start(bf16[16,1024]{1,0:T(8,128)(2,1)S(1)} %collective-permute-done.5), channel_id=1, source_target_pairs={{0,480},{32,0},{64,32},{96,64},{128,96},{160,128},{192,160},{224,1... | collective-permute-start | bytes 98312 | tf_op jit(solution)/shard_map/ppermute | solution.py:29
  194.2 7.1 %collective-permute-start.8 = (bf16[16,1024]{1,0:T(8,128)(2,1)S(1)}, bf16[16,1024]{1,0:T(8,128)(2,1)S(1)}, u32[]{:S(2)}, u32[]{:S(2)}) collective-permute-start(bf16[16,1024]{1,0:T(8,128)(2,1)S(1)} %collective-permute-done.6), channel_id=1, source_target_pairs={{0,32},{32,64},{64,96},{96,128},{128,160},{160,192},{192,224},{224... | collective-permute-start | bytes 98312 | tf_op jit(solution)/shard_map/ppermute | solution.py:24
  196.2 7.1 %collective-permute-start.9 = (bf16[16,1024]{1,0:T(8,128)(2,1)S(1)}, bf16[16,1024]{1,0:T(8,128)(2,1)S(1)}, u32[]{:S(2)}, u32[]{:S(2)}) collective-permute-start(bf16[16,1024]{1,0:T(8,128)(2,1)S(1)} %collective-permute-done.7), channel_id=1, source_target_pairs={{0,480},{32,0},{64,32},{96,64},{128,96},{160,128},{192,160},{224,1... | collective-permute-start | bytes 98312 | tf_op jit(solution)/shard_map/ppermute | solution.py:29
  201.4 7.1 %collective-permute-start.10 = (bf16[16,1024]{1,0:T(8,128)(2,1)S(1)}, bf16[16,1024]{1,0:T(8,128)(2,1)S(1)}, u32[]{:S(2)}, u32[]{:S(2)}) collective-permute-start(bf16[16,1024]{1,0:T(8,128)(2,1)S(1)} %collective-permute-done.8), channel_id=1, source_target_pairs={{0,32},{32,64},{64,96},{96,128},{128,160},{160,192},{192,224},{224... | collective-permute-start | bytes 98312 | tf_op jit(solution)/shard_map/ppermute | solution.py:24
  203.3 7.1 %collective-permute-start.11 = (bf16[16,1024]{1,0:T(8,128)(2,1)S(1)}, bf16[16,1024]{1,0:T(8,128)(2,1)S(1)}, u32[]{:S(2)}, u32[]{:S(2)}) collective-permute-start(bf16[16,1024]{1,0:T(8,128)(2,1)S(1)} %collective-permute-done.9), channel_id=1, source_target_pairs={{0,480},{32,0},{64,32},{96,64},{128,96},{160,128},{192,160},{224,1... | collective-permute-start | bytes 98312 | tf_op jit(solution)/shard_map/ppermute | solution.py:29
  208.5 7.1 %collective-permute-start.12 = (bf16[16,1024]{1,0:T(8,128)(2,1)S(1)}, bf16[16,1024]{1,0:T(8,128)(2,1)S(1)}, u32[]{:S(2)}, u32[]{:S(2)}) collective-permute-start(bf16[16,1024]{1,0:T(8,128)(2,1)S(1)} %collective-permute-done.10), channel_id=1, source_target_pairs={{0,32},{32,64},{64,96},{96,128},{128,160},{160,192},{192,224},{224... | collective-permute-start | bytes 98312 | tf_op jit(solution)/shard_map/ppermute | solution.py:24
  210.4 7.1 %collective-permute-start.13 = (bf16[16,1024]{1,0:T(8,128)(2,1)S(1)}, bf16[16,1024]{1,0:T(8,128)(2,1)S(1)}, u32[]{:S(2)}, u32[]{:S(2)}) collective-permute-start(bf16[16,1024]{1,0:T(8,128)(2,1)S(1)} %collective-permute-done.11), channel_id=1, source_target_pairs={{0,480},{32,0},{64,32},{96,64},{128,96},{160,128},{192,160},{224,1... | collective-permute-start | bytes 98312 | tf_op jit(solution)/shard_map/ppermute | solution.py:29
  215.6 7.0 %collective-permute-start.14 = (bf16[16,1024]{1,0:T(8,128)(2,1)S(1)}, bf16[16,1024]{1,0:T(8,128)(2,1)S(1)}, u32[]{:S(2)}, u32[]{:S(2)}) collective-permute-start(bf16[16,1024]{1,0:T(8,128)(2,1)S(1)} %collective-permute-done.12), channel_id=1, source_target_pairs={{0,32},{32,64},{64,96},{96,128},{128,160},{160,192},{192,224},{224... | collective-permute-start | bytes 98312 | tf_op jit(solution)/shard_map/ppermute | solution.py:24
  222.6 1.0 copy-start.1
Sparse Core Ops, SparseCore 0:
  10.8 78.2 reduce-scatter.1
